TPU v7x, 512 devices: a whole 4x4x16 slice. The times are simulated.
512 devices in a mesh: dp: 8 (over x, y_lo), tm: 64 (over z, y_hi, core).
Axes of the slice: x: 4, y: 4 (y_hi: 2, y_lo: 2; y = y_hi * 2 + y_lo), z: 16, core: 2. Of those that a mesh axis runs over, the one named last changes fastest.
Arguments:
- features: bfloat16 [8, 8192, 1536], P('dp', 'tm'), may hold values from -8 to 8
- start_noise: bfloat16 [8, 8192, 1536], P('dp', 'tm'), may hold values from -1 to 1
- cotangent: bfloat16 [8, 8192, 1536], P('dp', 'tm'), may hold values from -0.0234375 to 0.0234375
- in_weight: bfloat16 [3072, 1536], P('tm'), may hold values from -0.15625 to 0.15625
- kernel: float32 [31, 1536], replicated, may hold values from -1 to 1
- bn_gain: float32 [1536], replicated, may hold values from 0.25 to 1.75
- bn_shift: float32 [1536], replicated, may hold values from -1 to 1
- ends: int32 [8], replicated, may hold values from 4096 to 8192
Outputs:
- perturbation: float32 [8, 8192, 1536], P('dp', 'tm')
- grad_kernel: float32 [31, 1536], P(None, 'tm')
- grad_norm: float32 [2, 1536], P(None, 'tm')
Inputs may be any that keep to these rules, and one draw needn't show every extreme that they name: `ends`: frames at or after an utterance's end are padding.
All inputs are finite; a program needn't handle non-finite values.
Results may differ from a plain program's by a relative error of at most 0.0059.
Values may be sent and summed in bfloat16 or wider, within the bound.
A program may use at most 128 MiB of HBM per device.

v0:
```python
import jax
import jax.numpy as jnp
from jax import lax
from jax.sharding import PartitionSpec as P

ASCENT = 2
noise_scale = 0.5
ascent_rate = 0.5
layer_epsilon = 1e-05
batch_epsilon = 1e-05
ascent_epsilon = 1e-06


def normalize(summed):
    centre = summed - jnp.mean(summed, axis=-1, keepdims=True)
    inverse = lax.rsqrt(jnp.mean(centre * centre, axis=-1, keepdims=True) + layer_epsilon)
    return (centre * inverse, inverse)


def lane_conv_forward(padded, kernel, out_length):
    result = jnp.zeros((padded.shape[0], out_length), jnp.float32)
    for offset in range(kernel.shape[0]):
        result = result + kernel[offset][:, None] * padded[:, offset : offset + out_length].astype(
            jnp.float32
        )
    return result


def lane_conv_input_grad(padded, kernel, out_length):
    tap_span = kernel.shape[0] - 1
    result = jnp.zeros((padded.shape[0], out_length), jnp.float32)
    for offset in range(kernel.shape[0]):
        start_col = tap_span - offset
        result = result + kernel[offset][:, None] * padded[
            :, start_col : start_col + out_length
        ].astype(jnp.float32)
    return result


def lane_kernel_grad(grad_bf, padded, out_length):
    grad_float = grad_bf.astype(jnp.float32)
    rows_list = []
    for offset in range(padded.shape[1] - out_length + 1):
        rows_list.append(
            jnp.sum(
                grad_float * padded[:, offset : offset + out_length].astype(jnp.float32), axis=1
            )
        )
    return jnp.stack(rows_list)


def reduce_kernel(partial_grad):
    return lax.psum(partial_grad, "dp")


def on_device(features, start_noise, cotangent, in_weight, kernel, bn_gain, bn_shift, ends):
    frame_rows = features.shape[1]
    model_width = features.shape[2]
    tap_count = kernel.shape[0]
    half_span = (tap_count - 1) // 2
    shard_count = lax.axis_size("tm")
    shard_index = lax.axis_index("tm")
    group_index = lax.axis_index("dp")
    slice_width = model_width // shard_count
    all_frames = frame_rows * shard_count
    utter_end = lax.dynamic_index_in_dim(ends, group_index, 0, keepdims=False)
    live_count = jnp.sum(ends).astype(jnp.float32)
    utter_length = utter_end.astype(jnp.float32)
    frame_ids = shard_index * frame_rows + jnp.arange(frame_rows, dtype=jnp.int32)
    live_frames = (frame_ids < utter_end).astype(jnp.float32)
    live_whole = (jnp.arange(all_frames, dtype=jnp.int32) < utter_end).astype(jnp.float32)
    channel_start = shard_index * slice_width
    kernel_slice = lax.dynamic_slice_in_dim(kernel, channel_start, slice_width, 1)
    gain_slice = lax.dynamic_slice_in_dim(bn_gain, channel_start, slice_width, 0)
    shift_slice = lax.dynamic_slice_in_dim(bn_shift, channel_start, slice_width, 0)
    weight_full = lax.all_gather(in_weight, "tm", axis=0, tiled=True)
    inputs = features[0].astype(jnp.float32)
    perturbation = noise_scale * start_noise[0].astype(jnp.float32) * live_frames[:, None]
    cot_channels = lax.all_to_all(
        jnp.transpose(cotangent[0])[None], "tm", split_axis=1, concat_axis=2, tiled=True
    )[0]
    upstream = live_whole[None, :] * cot_channels.astype(jnp.float32) / ASCENT
    kernel_total = jnp.zeros((tap_count, slice_width), jnp.float32)
    norm_total = jnp.zeros((2, slice_width), jnp.float32)
    for ascent_step in range(ASCENT):
        summed = inputs + perturbation
        normed, inverse = normalize(summed)
        hidden = lax.dot_general(
            normed.astype(jnp.bfloat16),
            weight_full,
            (((1,), (1,)), ((), ())),
            preferred_element_type=jnp.float32,
        )
        value_half = hidden[:, :model_width]
        gate_half = jax.nn.sigmoid(hidden[:, model_width:])
        glu = (value_half * gate_half * live_frames[:, None]).astype(jnp.bfloat16)
        glu_local = lax.all_to_all(
            jnp.transpose(glu)[None], "tm", split_axis=1, concat_axis=2, tiled=True
        )[0]
        padded = jnp.pad(glu_local, ((0, 0), (half_span, half_span)))
        conv_out = lane_conv_forward(padded, kernel_slice, all_frames)
        live_mask = live_whole[None, :]
        batch_mean = lax.psum(jnp.sum(live_mask * conv_out, axis=1), "dp") / live_count
        centred = conv_out - batch_mean[:, None]
        variance = lax.psum(jnp.sum(live_mask * centred * centred, axis=1), "dp") / live_count
        inv_std = lax.rsqrt(variance + batch_epsilon)[:, None]
        gain_now, shift_now = (gain_slice[:, None], shift_slice[:, None])
        scaled = centred * inv_std
        pre_act = gain_now * scaled + shift_now
        pre_sigmoid = jax.nn.sigmoid(pre_act)
        grad_pre = upstream * pre_sigmoid * (1.0 + pre_act * (1.0 - pre_sigmoid))
        shift_sum, gain_sum = lax.psum(
            (jnp.sum(grad_pre, axis=1), jnp.sum(grad_pre * scaled, axis=1)), "dp"
        )
        norm_total = norm_total + jnp.stack([gain_sum, shift_sum])
        grad_conv = (
            live_mask
            * inv_std
            * gain_now
            * (grad_pre - (shift_sum[:, None] + scaled * gain_sum[:, None]) / live_count)
        ).astype(jnp.bfloat16)
        kernel_part = lane_kernel_grad(grad_conv, padded, all_frames)
        kernel_total = kernel_total + reduce_kernel(kernel_part)
        if ascent_step + 1 < ASCENT:
            grad_pad = jnp.pad(grad_conv, ((0, 0), (half_span, half_span)))
            grad_local = (
                lane_conv_input_grad(grad_pad, kernel_slice, all_frames) * live_mask
            ).astype(jnp.bfloat16)
            grad_glu = jnp.transpose(
                lax.all_to_all(grad_local[None], "tm", split_axis=2, concat_axis=1, tiled=True)[0]
            )
            grad_float = grad_glu.astype(jnp.float32)
            grad_hidden = jnp.concatenate(
                [grad_float * gate_half, grad_float * value_half * gate_half * (1.0 - gate_half)],
                axis=1,
            ).astype(jnp.bfloat16)
            grad_normed = jnp.dot(grad_hidden, weight_full, preferred_element_type=jnp.float32)
            grad_sum = inverse * (
                grad_normed
                - jnp.mean(grad_normed, axis=-1, keepdims=True)
                - normed * jnp.mean(grad_normed * normed, axis=-1, keepdims=True)
            )
            direction = live_frames[:, None] * grad_sum
            square_total = lax.psum(jnp.sum(direction * direction), "tm")
            perturbation = perturbation + direction * (
                ascent_rate
                * jnp.sqrt(utter_length * model_width)
                / (jnp.sqrt(square_total) + ascent_epsilon)
            )
    return (perturbation[None], kernel_total, norm_total)


def solution(mesh):
    return jax.shard_map(
        on_device,
        mesh=mesh,
        in_specs=(
            P("dp", "tm", None),
            P("dp", "tm", None),
            P("dp", "tm", None),
            P("tm", None),
            P(),
            P(),
            P(),
            P(),
        ),
        out_specs=(P("dp", "tm", None), P(None, "tm"), P(None, "tm")),
        check_vma=False,
    )
```

profile of v0, /device:TPU:16, one launch (start us, length us, event | category | flops | bytes accessed | tf_op | source)
XLA Modules:
  0.0 742.7 jit_solution(14522599243444606599)
XLA Ops:
  15.8 8.8 %reduce.1 = bf16[1536,128]{1,0:T(8,128)(2,1)S(1)} reduce(bf16[1536,1,128]{2,1,0:T(2,128)(2,1)S(1)} %bitcast.268, bf16[]{:T(256)} %broadcast.129), dimensions={1}, to_apply=%bitcast.247.reduce_sub_computation | reduce | bytes 786434
  25.5 18.9 %all-to-all-start.1 = ((bf16[64,2,1536]{2,1,0:T(2,128)(2,1)}), bf16[64,2,1536]{2,1,0:T(2,128)(2,1)S(1)}, u32[]{:S(2)}, u32[]{:S(2)}) async-start(bf16[64,2,1536]{2,1,0:T(2,128)(2,1)} %reshape.112), calls=%async_computation.1 | async-start | bytes 786432 | tf_op jit(solution)/shard_map/all_to_all | solution.py:79
  47.0 140.4 %all-gather.2.cloned.1.call-done = bf16[3072,1536]{1,0:T(8,128)(2,1)} async-done(((bf16[48,1536]{1,0:T(8,128)(2,1)}), bf16[3072,1536]{1,0:T(8,128)(2,1)}) %all-gather.2.cloned.1.call-update) | async-done | bytes 9437200 | tf_op jit(solution)/shard_map/all_gather | solution.py:76
  187.4 6.9 fusion.162
  197.5 9.5 %reduce = bf16[1536,128]{1,0:T(8,128)(2,1)} reduce(bf16[1536,1,128]{2,1,0:T(2,128)(2,1)S(1)} %bitcast.270, bf16[]{:T(256)} %broadcast.129), dimensions={1}, to_apply=%bitcast.227.reduce_sub_computation | reduce | bytes 786434
  208.8 11.1 %all-to-all-start = ((bf16[64,2,1536]{2,1,0:T(2,128)(2,1)}), bf16[64,2,1536]{2,1,0:T(2,128)(2,1)}, u32[]{:S(2)}, u32[]{:S(2)}) async-start(bf16[64,2,1536]{2,1,0:T(2,128)(2,1)} %reshape.114), calls=%async_computation | async-start | bytes 786432 | tf_op jit(solution)/shard_map/all_to_all | solution.py:97
  230.5 17.4 %all-to-all-done = bf16[64,2,1536]{2,1,0:T(2,128)(2,1)} async-done(((bf16[64,2,1536]{2,1,0:T(2,128)(2,1)}), bf16[64,2,1536]{2,1,0:T(2,128)(2,1)}, u32[]{:S(2)}, u32[]{:S(2)}) %all-to-all-start) | async-done | bytes 393248 | tf_op jit(solution)/shard_map/all_to_all | solution.py:97
  257.5 20.7 %psum.77 = f32[24]{0:T(128)} all-reduce(f32[24]{0:T(128)} %get-tuple-element.100), channel_id=1, replica_groups=mesh['dp'=8,'tm'=64] {'dp'}, use_global_device_ids=true, to_apply=%region_3.4 | all-reduce | flops 24 | bytes 192 | tf_op jit(solution)/shard_map/psum | solution.py:103
  281.0 16.6 %psum.78 = f32[24]{0:T(128)} all-reduce(f32[24]{0:T(128)} %fusion.60), channel_id=1, replica_groups=mesh['dp'=8,'tm'=64] {'dp'}, use_global_device_ids=true, to_apply=%region_6.7 | all-reduce | flops 24 | bytes 192 | tf_op jit(solution)/shard_map/psum | solution.py:105
  302.2 18.9 %all-reduce.4 = (f32[24]{0:T(128)}, f32[24]{0:T(128)}) all-reduce(f32[24]{0:T(128)} %get-tuple-element.83, f32[24]{0:T(128)} %get-tuple-element.82), channel_id=1, replica_groups=mesh['dp'=8,'tm'=64] {'dp'}, use_global_device_ids=true, to_apply=%region_10.11 | all-reduce | flops 48 | bytes 384 | tf_op jit(solution)/shard_map/psum | solution.py:112
  330.4 6.7 copy.52
  337.1 46.5 %reduce.2 = bf16[8192,24]{1,0:T(8,128)(2,1)} reduce(bf16[8192,1,24]{2,1,0:T(2,128)(2,1)} %bitcast.248, bf16[]{:T(256)} %broadcast.129), dimensions={1}, to_apply=%bitcast.229.reduce_sub_computation | reduce | bytes 786434
  395.2 27.1 %all-to-all-done.2 = bf16[64,2,1536]{2,1,0:T(2,128)(2,1)S(1)} async-done(((bf16[64,2,1536]{2,1,0:T(2,128)(2,1)}), bf16[64,2,1536]{2,1,0:T(2,128)(2,1)S(1)}, u32[]{:S(2)}, u32[]{:S(2)}) %all-to-all-start.2) | async-done | bytes 393248 | tf_op jit(solution)/shard_map/all_to_all | solution.py:130
  422.3 8.9 %reshape.117 = bf16[8192,1,24]{2,1,0:T(2,128)(2,1)} reshape(bf16[64,2,1536]{2,1,0:T(2,128)(2,1)S(1)} %all-to-all-done.2) | data formatting | bytes 786432
  431.2 8.0 %copy.53 = bf16[1,24,8192]{2,1,0:T(8,128)(2,1)S(1)} copy(bf16[1,24,8192]{1,0,2:T(2,128)(2,1)} %bitcast.249) | data formatting | bytes 786432 | tf_op jit(solution)/shard_map/all_to_all | solution.py:130
  449.0 125.4 %psum.81 = f32[]{:T(128)} all-reduce(f32[]{:T(128)} %get-tuple-element.97), channel_id=1, replica_groups=mesh['dp'=8,'tm'=64] {'tm'}, use_global_device_ids=true, to_apply=%region_14.15 | all-reduce | flops 1 | bytes 8 | tf_op jit(solution)/shard_map/psum | solution.py:144
  576.5 6.8 fusion.165
  584.2 8.8 %reduce.3 = bf16[1536,128]{1,0:T(8,128)(2,1)S(1)} reduce(bf16[1536,1,128]{2,1,0:T(2,128)(2,1)S(1)} %bitcast.269, bf16[]{:T(256)} %broadcast.129), dimensions={1}, to_apply=%bitcast.231.reduce_sub_computation | reduce | bytes 786434
  593.8 11.3 %all-to-all-start.3 = ((bf16[64,2,1536]{2,1,0:T(2,128)(2,1)}), bf16[64,2,1536]{2,1,0:T(2,128)(2,1)S(1)}, u32[]{:S(2)}, u32[]{:S(2)}) async-start(bf16[64,2,1536]{2,1,0:T(2,128)(2,1)} %reshape.118), calls=%async_computation.3 | async-start | bytes 786432 | tf_op jit(solution)/shard_map/all_to_all | solution.py:97
  609.0 24.0 %all-to-all-done.3 = bf16[64,2,1536]{2,1,0:T(2,128)(2,1)S(1)} async-done(((bf16[64,2,1536]{2,1,0:T(2,128)(2,1)}), bf16[64,2,1536]{2,1,0:T(2,128)(2,1)S(1)}, u32[]{:S(2)}, u32[]{:S(2)}) %all-to-all-start.3) | async-done | bytes 393248 | tf_op jit(solution)/shard_map/all_to_all | solution.py:97
  639.8 16.1 %psum.83 = f32[24]{0:T(128)S(1)} all-reduce(f32[24]{0:T(128)} %get-tuple-element.92), channel_id=1, replica_groups=mesh['dp'=8,'tm'=64] {'dp'}, use_global_device_ids=true, to_apply=%region_50.51 | all-reduce | flops 24 | bytes 192 | tf_op jit(solution)/shard_map/psum | solution.py:103
  656.9 18.0 %psum.84 = f32[24]{0:T(128)S(1)} all-reduce(f32[24]{0:T(128)S(1)} %fusion.61), channel_id=1, replica_groups=mesh['dp'=8,'tm'=64] {'dp'}, use_global_device_ids=true, to_apply=%region_52.53 | all-reduce | flops 24 | bytes 192 | tf_op jit(solution)/shard_map/psum | solution.py:105
  678.1 16.3 %all-reduce.3 = (f32[24]{0:T(128)S(1)}, f32[24]{0:T(128)S(1)}) all-reduce(f32[24]{0:T(128)} %get-tuple-element.49, f32[24]{0:T(128)} %get-tuple-element.48), channel_id=1, replica_groups=mesh['dp'=8,'tm'=64] {'dp'}, use_global_device_ids=true, to_apply=%region_56.57 | all-reduce | flops 48 | bytes 384 | tf_op jit(solution)/shard_map/psum | solution.py:112
  701.9 32.5 %psum.88 = f32[31,24]{1,0:T(8,128)S(1)} all-reduce(f32[31,24]{1,0:T(8,128)S(1)} %add.520), channel_id=1, replica_groups=mesh['dp'=8,'tm'=64] {'dp'}, use_global_device_ids=true, to_apply=%region_46.47 | all-reduce | flops 744 | bytes 5952 | tf_op jit(solution)/shard_map/psum | solution.py:53
  (170 shorter events, 99.9 us)
Async XLA Ops:
  7.2 37.2 %copy-start.46 = (s32[8]{0:T(128)S(1)}, s32[8]{0:T(128)}, u32[]{:S(2)}) copy-start(s32[8]{0:T(128)} %param.15) | copy-start | bytes 100
  7.2 38.5 %copy-start.1 = (bf16[1,128,1536]{2,1,0:T(8,128)(2,1)S(1)}, bf16[1,128,1536]{2,1,0:T(8,128)(2,1)}, u32[]{:S(2)}) copy-start(bf16[1,128,1536]{2,1,0:T(8,128)(2,1)} %param.8) | copy-start | bytes 1179652
  7.2 38.5 %copy-start = (bf16[1,128,1536]{2,1,0:T(8,128)(2,1)S(1)}, bf16[1,128,1536]{2,1,0:T(8,128)(2,1)}, u32[]{:S(2)}) copy-start(bf16[1,128,1536]{2,1,0:T(8,128)(2,1)} %param.9) | copy-start | bytes 1179652
  7.2 180.2 %all-gather.2.cloned.1.call-start = ((), (), s32[]{:S(2)}) async-start(), calls=%async_computation.4 | async-start | bytes 9584640 | tf_op jit(solution)/shard_map/all_gather | solution.py:76
  25.5 183.3 %all-to-all-start.1 = ((bf16[64,2,1536]{2,1,0:T(2,128)(2,1)}), bf16[64,2,1536]{2,1,0:T(2,128)(2,1)S(1)}, u32[]{:S(2)}, u32[]{:S(2)}) async-start(bf16[64,2,1536]{2,1,0:T(2,128)(2,1)} %reshape.112), calls=%async_computation.1 | async-start | bytes 786432 | tf_op jit(solution)/shard_map/all_to_all | solution.py:79
  46.0 148.3 %copy-start.11 = (f32[128]{0:T(128)}, f32[128]{0:T(128)S(1)}, u32[]{:S(2)}) copy-start(f32[128]{0:T(128)S(1)} %broadcast_multiply_fusion.3) | copy-start | bytes 1540
  46.6 147.7 %copy-start.8 = (f32[128]{0:T(128)}, f32[128]{0:T(128)S(1)}, u32[]{:S(2)}) copy-start(f32[128]{0:T(128)S(1)} %compare_convert_fusion) | copy-start | bytes 1540
  47.0 147.3 %copy-start.40 = (f32[128]{0:T(128)}, f32[128]{0:T(128)S(1)}, u32[]{:S(2)}) copy-start(f32[128]{0:T(128)S(1)} %add_rsqrt_fusion.3) | copy-start | bytes 1540
  208.8 39.0 %all-to-all-start = ((bf16[64,2,1536]{2,1,0:T(2,128)(2,1)}), bf16[64,2,1536]{2,1,0:T(2,128)(2,1)}, u32[]{:S(2)}, u32[]{:S(2)}) async-start(bf16[64,2,1536]{2,1,0:T(2,128)(2,1)} %reshape.114), calls=%async_computation | async-start | bytes 786432 | tf_op jit(solution)/shard_map/all_to_all | solution.py:97
  388.5 33.8 %all-to-all-start.2 = ((bf16[64,2,1536]{2,1,0:T(2,128)(2,1)}), bf16[64,2,1536]{2,1,0:T(2,128)(2,1)S(1)}, u32[]{:S(2)}, u32[]{:S(2)}) async-start(bf16[64,2,1536]{2,1,0:T(2,128)(2,1)} %reshape.116), calls=%async_computation.2 | async-start | bytes 786432 | tf_op jit(solution)/shard_map/all_to_all | solution.py:130
  584.2 49.6 %copy-start.7 = (f32[24]{0:T(128)S(1)}, f32[24]{0:T(128)}, u32[]{:S(2)}) copy-start(f32[24]{0:T(128)} %get-tuple-element.108) | copy-start | bytes 292
  593.8 81.0 %copy-start.4 = (f32[1,24,64,128]{3,2,1,0:T(8,128)S(1)}, f32[1,24,64,128]{3,2,1,0:T(8,128)}, u32[]{:S(2)}) copy-start(f32[1,24,64,128]{3,2,1,0:T(8,128)} %copy.51) | copy-start | bytes 2359300
  593.8 39.2 %all-to-all-start.3 = ((bf16[64,2,1536]{2,1,0:T(2,128)(2,1)}), bf16[64,2,1536]{2,1,0:T(2,128)(2,1)S(1)}, u32[]{:S(2)}, u32[]{:S(2)}) async-start(bf16[64,2,1536]{2,1,0:T(2,128)(2,1)} %reshape.118), calls=%async_computation.3 | async-start | bytes 786432 | tf_op jit(solution)/shard_map/all_to_all | solution.py:97
  633.7 66.2 %copy-start.6 = (bf16[1,24,64,128]{3,2,1,0:T(8,128)(2,1)S(1)}, bf16[1,24,64,128]{3,2,1,0:T(8,128)(2,1)}, u32[]{:S(2)}) copy-start(bf16[1,24,64,128]{3,2,1,0:T(8,128)(2,1)} %copy-done.5) | copy-start | bytes 1179652
  674.9 26.6 %copy-start.13 = (f32[24]{0:T(128)S(1)}, f32[24]{0:T(128)}, u32[]{:S(2)}) copy-start(f32[24]{0:T(128)} %get-tuple-element.50) | copy-start | bytes 292
  674.9 26.6 %copy-start.14 = (f32[24]{0:T(128)S(1)}, f32[24]{0:T(128)}, u32[]{:S(2)}) copy-start(f32[24]{0:T(128)} %get-tuple-element.51) | copy-start | bytes 292
  674.9 26.6 %copy-start.15 = (f32[24]{0:T(128)S(1)}, f32[24]{0:T(128)}, u32[]{:S(2)}) copy-start(f32[24]{0:T(128)} %get-tuple-element.52) | copy-start | bytes 292
  677.9 23.7 %copy-start.19 = (f32[24]{0:T(128)S(1)}, f32[24]{0:T(128)}, u32[]{:S(2)}) copy-start(f32[24]{0:T(128)} %get-tuple-element.56) | copy-start | bytes 292
  677.9 23.7 %copy-start.20 = (f32[24]{0:T(128)S(1)}, f32[24]{0:T(128)}, u32[]{:S(2)}) copy-start(f32[24]{0:T(128)} %get-tuple-element.57) | copy-start | bytes 292
  677.9 23.7 %copy-start.21 = (f32[24]{0:T(128)S(1)}, f32[24]{0:T(128)}, u32[]{:S(2)}) copy-start(f32[24]{0:T(128)} %get-tuple-element.58) | copy-start | bytes 292
  677.9 23.7 %copy-start.22 = (f32[24]{0:T(128)S(1)}, f32[24]{0:T(128)}, u32[]{:S(2)}) copy-start(f32[24]{0:T(128)} %get-tuple-element.59) | copy-start | bytes 292
  677.9 23.7 %copy-start.23 = (f32[24]{0:T(128)S(1)}, f32[24]{0:T(128)}, u32[]{:S(2)}) copy-start(f32[24]{0:T(128)} %get-tuple-element.60) | copy-start | bytes 292
  678.1 56.9 %copy-start.44 = (f32[24]{0:T(128)S(1)}, f32[24]{0:T(128)}, u32[]{:S(2)}) copy-start(f32[24]{0:T(128)} %get-tuple-element.88) | copy-start | bytes 292
  678.1 56.9 %copy-start.45 = (f32[24]{0:T(128)S(1)}, f32[24]{0:T(128)}, u32[]{:S(2)}) copy-start(f32[24]{0:T(128)} %get-tuple-element.89) | copy-start | bytes 292
  (28 other events, 493.6 us)
Sparse Core Ops, SparseCore 0:
  11.3 176.0 all-gather.1
where the time goes:
time: 750 us; the launch traced here: 743 us
  blocking collectives  264 us (35%)
  waiting for transfers between devices  210 us (28%)
  other arithmetic  125 us (17%)
  local copies, waits for them, and re-layouts  60.1 us (8%)
  starting transfers between devices  47.4 us (6%)
  matrix products  19 us (3%)
  between operations  17.2 us (2%)
    all_gather x1, waiting for transfers between devices, on_device(): weight_full = lax.all_gather(in_weight, 'tm', axis=0, tiled=True)  140 us
    psum x1, blocking collectives, on_device(): square_total = lax.psum(jnp.sum(direction * direction), 'tm')  125 us
    unnamed x5, other arithmetic  73.6 us
    all_to_all x2, waiting for transfers between devices, on_device(): lax.all_to_all(jnp.transpose(glu)[None], 'tm', split_axis=1, concat_axis=...  41.4 us
    psum x2, blocking collectives, on_device(): lax.psum(jnp.sum(live_mask * conv_out, axis=1), 'dp') / live_count  36.8 us
    psum x2, blocking collectives, on_device(): lax.psum((jnp.sum(grad_pre, axis=1), jnp.sum(grad_pre * scaled, axis=1)),...  35.2 us
    psum x2, blocking collectives, on_device(): lax.psum(jnp.sum(live_mask * centred * centred, axis=1), 'dp') / live_count  34.5 us
    psum x1, blocking collectives, reduce_kernel(): return lax.psum(partial_grad, 'dp')  32.5 us
  transfers between devices with their start and end apart: 5, of which 4 were waited for; matrix products, arithmetic and copies ran while one was open for 7% of the time, Pallas kernels for 0%

commit v1 on v0

--- a/solution.py
+++ b/solution.py
@@ -73,7 +73,9 @@
     kernel_slice = lax.dynamic_slice_in_dim(kernel, channel_start, slice_width, 1)
     gain_slice = lax.dynamic_slice_in_dim(bn_gain, channel_start, slice_width, 0)
     shift_slice = lax.dynamic_slice_in_dim(bn_shift, channel_start, slice_width, 0)
-    weight_full = lax.all_gather(in_weight, "tm", axis=0, tiled=True)
+    weight_full = jnp.concatenate(
+        lax.all_to_all(jnp.stack([in_weight] * lax.axis_size("tm")), "tm", 0, 0), axis=0
+    )
     inputs = features[0].astype(jnp.float32)
     perturbation = noise_scale * start_noise[0].astype(jnp.float32) * live_frames[:, None]
     cot_channels = lax.all_to_all(

time: 750 us -> 1010 us (1.35)
  waiting for transfers between devices: 210 us -> 471 us
  between operations: 17.2 us -> 3.85 us
    all_to_all x0 -> x1, waiting for transfers between devices: none -> 397 us  [on_device(): lax.all_to_all(jnp.stack([in_weight] * lax.axis_size('tm')), 'tm', 0, 0)]
    all_gather x1 -> x0, waiting for transfers between devices: 140 us -> none  [on_device(): weight_full = lax.all_gather(in_weight, 'tm', axis=0, tiled=True)]
    all_to_all x0 -> x1, starting transfers between devices: none -> 18.9 us  [on_device(): lax.all_to_all(jnp.stack([in_weight] * lax.axis_size('tm')), 'tm', 0, 0)]
    all_to_all x1, starting transfers between devices: 18.9 us -> 5.65 us  [on_device(): lax.all_to_all(jnp.transpose(cotangent[0])[None], 'tm', split_axis=1, con...]
    unnamed x110 -> x112, local copies, waits for them, and re-layouts: 26.4 us -> 25.5 us
  transfers between devices with their start and end apart: 5 -> 5, of which waited for: 4 -> 5; matrix products, arithmetic and copies ran while one was open for 7% -> 5% of each run, Pallas kernels for 0% -> 0%
where the time goes in v1:
time: 1010 us; the launch traced here: 999 us
  waiting for transfers between devices  471 us (47%)
  blocking collectives  264 us (26%)
  other arithmetic  125 us (12%)
  local copies, waits for them, and re-layouts  64.5 us (6%)
  starting transfers between devices  51.8 us (5%)
  matrix products  19 us (2%)
    all_to_all x1, waiting for transfers between devices, on_device(): lax.all_to_all(jnp.stack([in_weight] * lax.axis_size('tm')), 'tm', 0, 0)  397 us
    psum x1, blocking collectives, on_device(): square_total = lax.psum(jnp.sum(direction * direction), 'tm')  125 us
    unnamed x5, other arithmetic  73.9 us
    all_to_all x2, waiting for transfers between devices, on_device(): lax.all_to_all(jnp.transpose(glu)[None], 'tm', split_axis=1, concat_axis=...  41.6 us
    psum x2, blocking collectives, on_device(): lax.psum(jnp.sum(live_mask * conv_out, axis=1), 'dp') / live_count  36.1 us
    psum x2, blocking collectives, on_device(): lax.psum((jnp.sum(grad_pre, axis=1), jnp.sum(grad_pre * scaled, axis=1)),...  35.2 us
    psum x2, blocking collectives, on_device(): lax.psum(jnp.sum(live_mask * centred * centred, axis=1), 'dp') / live_count  34.5 us
    psum x1, blocking collectives, reduce_kernel(): return lax.psum(partial_grad, 'dp')  32.5 us
  transfers between devices with their start and end apart: 5, of which 5 were waited for; matrix products, arithmetic and copies ran while one was open for 5% of the time, Pallas kernels for 0%

profile of v1, /device:TPU:16, one launch (start us, length us, event | category | flops | bytes accessed | tf_op | source)
XLA Modules:
  0.0 999.5 jit_solution(7381033206506379327)
XLA Ops:
  6.3 18.9 %all-to-all-start = ((bf16[64,48,1536]{2,1,0:T(8,128)(2,1)}), bf16[64,48,1536]{2,1,0:T(8,128)(2,1)}, u32[]{:S(2)}, u32[]{:S(2)}) async-start(bf16[64,48,1536]{2,1,0:T(8,128)(2,1)} %stack.277), calls=%async_computation | async-start | bytes 18874368 | tf_op jit(solution)/shard_map/all_to_all | solution.py:77
  32.2 8.8 reduce.1
  43.5 397.3 %all-to-all-done = bf16[64,48,1536]{2,1,0:T(8,128)(2,1)} async-done(((bf16[64,48,1536]{2,1,0:T(8,128)(2,1)}), bf16[64,48,1536]{2,1,0:T(8,128)(2,1)}, u32[]{:S(2)}, u32[]{:S(2)}) %all-to-all-start) | async-done | bytes 9437216 | tf_op jit(solution)/shard_map/all_to_all | solution.py:77
  447.5 6.9 fusion.171
  457.6 9.6 reduce
  474.3 10.0 all-to-all-start.1
  494.5 17.6 %all-to-all-done.1 = bf16[64,2,1536]{2,1,0:T(2,128)(2,1)} async-done(((bf16[64,2,1536]{2,1,0:T(2,128)(2,1)}), bf16[64,2,1536]{2,1,0:T(2,128)(2,1)}, u32[]{:S(2)}, u32[]{:S(2)}) %all-to-all-start.1) | async-done | bytes 393248 | tf_op jit(solution)/shard_map/all_to_all | solution.py:99
  521.8 20.0 %psum.77 = f32[24]{0:T(128)} all-reduce(f32[24]{0:T(128)} %get-tuple-element.100), channel_id=1, replica_groups=mesh['dp'=8,'tm'=64] {'dp'}, use_global_device_ids=true, to_apply=%region_3.4 | all-reduce | flops 24 | bytes 192 | tf_op jit(solution)/shard_map/psum | solution.py:105
  544.6 16.6 %psum.78 = f32[24]{0:T(128)} all-reduce(f32[24]{0:T(128)} %fusion.67), channel_id=1, replica_groups=mesh['dp'=8,'tm'=64] {'dp'}, use_global_device_ids=true, to_apply=%region_6.7 | all-reduce | flops 24 | bytes 192 | tf_op jit(solution)/shard_map/psum | solution.py:107
  565.8 18.9 %all-reduce.4 = (f32[24]{0:T(128)}, f32[24]{0:T(128)}) all-reduce(f32[24]{0:T(128)} %get-tuple-element.83, f32[24]{0:T(128)} %get-tuple-element.82), channel_id=1, replica_groups=mesh['dp'=8,'tm'=64] {'dp'}, use_global_device_ids=true, to_apply=%region_10.11 | all-reduce | flops 48 | bytes 384 | tf_op jit(solution)/shard_map/psum | solution.py:114
  594.0 6.7 copy.52
  600.7 46.6 %reduce.2 = bf16[8192,24]{1,0:T(8,128)(2,1)} reduce(bf16[8192,1,24]{2,1,0:T(2,128)(2,1)} %bitcast.267, bf16[]{:T(256)} %broadcast.140), dimensions={1}, to_apply=%bitcast.248.reduce_sub_computation | reduce | bytes 786434
  658.7 27.1 %all-to-all-done.3 = bf16[64,2,1536]{2,1,0:T(2,128)(2,1)S(1)} async-done(((bf16[64,2,1536]{2,1,0:T(2,128)(2,1)}), bf16[64,2,1536]{2,1,0:T(2,128)(2,1)S(1)}, u32[]{:S(2)}, u32[]{:S(2)}) %all-to-all-start.3) | async-done | bytes 393248 | tf_op jit(solution)/shard_map/all_to_all | solution.py:132
  685.9 8.9 reshape.142
  694.8 8.0 copy.53
  712.6 125.4 %psum.81 = f32[]{:T(128)} all-reduce(f32[]{:T(128)} %get-tuple-element.97), channel_id=1, replica_groups=mesh['dp'=8,'tm'=64] {'tm'}, use_global_device_ids=true, to_apply=%region_14.15 | all-reduce | flops 1 | bytes 8 | tf_op jit(solution)/shard_map/psum | solution.py:146
  840.1 6.8 fusion.169
  847.8 8.8 reduce.3
  857.5 11.3 %all-to-all-start.4 = ((bf16[64,2,1536]{2,1,0:T(2,128)(2,1)}), bf16[64,2,1536]{2,1,0:T(2,128)(2,1)S(1)}, u32[]{:S(2)}, u32[]{:S(2)}) async-start(bf16[64,2,1536]{2,1,0:T(2,128)(2,1)} %reshape.143), calls=%async_computation.4 | async-start | bytes 786432 | tf_op jit(solution)/shard_map/all_to_all | solution.py:99
  872.7 24.0 %all-to-all-done.4 = bf16[64,2,1536]{2,1,0:T(2,128)(2,1)S(1)} async-done(((bf16[64,2,1536]{2,1,0:T(2,128)(2,1)}), bf16[64,2,1536]{2,1,0:T(2,128)(2,1)S(1)}, u32[]{:S(2)}, u32[]{:S(2)}) %all-to-all-start.4) | async-done | bytes 393248 | tf_op jit(solution)/shard_map/all_to_all | solution.py:99
  903.4 16.1 %psum.83 = f32[24]{0:T(128)S(1)} all-reduce(f32[24]{0:T(128)} %get-tuple-element.92), channel_id=1, replica_groups=mesh['dp'=8,'tm'=64] {'dp'}, use_global_device_ids=true, to_apply=%region_50.51 | all-reduce | flops 24 | bytes 192 | tf_op jit(solution)/shard_map/psum | solution.py:105
  920.5 18.0 %psum.84 = f32[24]{0:T(128)S(1)} all-reduce(f32[24]{0:T(128)S(1)} %fusion.68), channel_id=1, replica_groups=mesh['dp'=8,'tm'=64] {'dp'}, use_global_device_ids=true, to_apply=%region_52.53 | all-reduce | flops 24 | bytes 192 | tf_op jit(solution)/shard_map/psum | solution.py:107
  941.8 16.3 %all-reduce.3 = (f32[24]{0:T(128)S(1)}, f32[24]{0:T(128)S(1)}) all-reduce(f32[24]{0:T(128)} %get-tuple-element.49, f32[24]{0:T(128)} %get-tuple-element.48), channel_id=1, replica_groups=mesh['dp'=8,'tm'=64] {'dp'}, use_global_device_ids=true, to_apply=%region_56.57 | all-reduce | flops 48 | bytes 384 | tf_op jit(solution)/shard_map/psum | solution.py:114
  965.5 32.5 %psum.88 = f32[31,24]{1,0:T(8,128)S(1)} all-reduce(f32[31,24]{1,0:T(8,128)S(1)} %add.524), channel_id=1, replica_groups=mesh['dp'=8,'tm'=64] {'dp'}, use_global_device_ids=true, to_apply=%region_46.47 | all-reduce | flops 744 | bytes 5952 | tf_op jit(solution)/shard_map/psum | solution.py:53
  (172 shorter events, 114.6 us)
Async XLA Ops:
  6.3 35.6 %copy-start.47 = (s32[8]{0:T(128)S(1)}, s32[8]{0:T(128)}, u32[]{:S(2)}) copy-start(s32[8]{0:T(128)} %param.15) | copy-start | bytes 100
  6.3 434.5 %all-to-all-start = ((bf16[64,48,1536]{2,1,0:T(8,128)(2,1)}), bf16[64,48,1536]{2,1,0:T(8,128)(2,1)}, u32[]{:S(2)}, u32[]{:S(2)}) async-start(bf16[64,48,1536]{2,1,0:T(8,128)(2,1)} %stack.277), calls=%async_computation | async-start | bytes 18874368 | tf_op jit(solution)/shard_map/all_to_all | solution.py:77
  43.5 410.9 %copy-start.12 = (f32[128]{0:T(128)}, f32[128]{0:T(128)S(1)}, u32[]{:S(2)}) copy-start(f32[128]{0:T(128)S(1)} %broadcast_multiply_fusion.3) | copy-start | bytes 1540
  440.8 33.5 %all-to-all-start.2 = ((bf16[64,2,1536]{2,1,0:T(2,128)(2,1)}), bf16[64,2,1536]{2,1,0:T(2,128)(2,1)S(1)}, u32[]{:S(2)}, u32[]{:S(2)}) async-start(bf16[64,2,1536]{2,1,0:T(2,128)(2,1)} %reshape.137), calls=%async_computation.2 | async-start | bytes 786432 | tf_op jit(solution)/shard_map/all_to_all | solution.py:81
  474.3 37.9 %all-to-all-start.1 = ((bf16[64,2,1536]{2,1,0:T(2,128)(2,1)}), bf16[64,2,1536]{2,1,0:T(2,128)(2,1)}, u32[]{:S(2)}, u32[]{:S(2)}) async-start(bf16[64,2,1536]{2,1,0:T(2,128)(2,1)} %reshape.139), calls=%async_computation.1 | async-start | bytes 786432 | tf_op jit(solution)/shard_map/all_to_all | solution.py:99
  652.1 33.8 %all-to-all-start.3 = ((bf16[64,2,1536]{2,1,0:T(2,128)(2,1)}), bf16[64,2,1536]{2,1,0:T(2,128)(2,1)S(1)}, u32[]{:S(2)}, u32[]{:S(2)}) async-start(bf16[64,2,1536]{2,1,0:T(2,128)(2,1)} %reshape.141), calls=%async_computation.3 | async-start | bytes 786432 | tf_op jit(solution)/shard_map/all_to_all | solution.py:132
  847.7 49.6 %copy-start.8 = (f32[24]{0:T(128)S(1)}, f32[24]{0:T(128)}, u32[]{:S(2)}) copy-start(f32[24]{0:T(128)} %get-tuple-element.108) | copy-start | bytes 292
  857.5 81.0 %copy-start.4 = (f32[1,24,64,128]{3,2,1,0:T(8,128)S(1)}, f32[1,24,64,128]{3,2,1,0:T(8,128)}, u32[]{:S(2)}) copy-start(f32[1,24,64,128]{3,2,1,0:T(8,128)} %copy.51) | copy-start | bytes 2359300
  857.5 39.2 %all-to-all-start.4 = ((bf16[64,2,1536]{2,1,0:T(2,128)(2,1)}), bf16[64,2,1536]{2,1,0:T(2,128)(2,1)S(1)}, u32[]{:S(2)}, u32[]{:S(2)}) async-start(bf16[64,2,1536]{2,1,0:T(2,128)(2,1)} %reshape.143), calls=%async_computation.4 | async-start | bytes 786432 | tf_op jit(solution)/shard_map/all_to_all | solution.py:99
  897.4 66.2 %copy-start.6 = (bf16[1,24,64,128]{3,2,1,0:T(8,128)(2,1)S(1)}, bf16[1,24,64,128]{3,2,1,0:T(8,128)(2,1)}, u32[]{:S(2)}) copy-start(bf16[1,24,64,128]{3,2,1,0:T(8,128)(2,1)} %copy-done.5) | copy-start | bytes 1179652
  938.5 26.6 %copy-start.14 = (f32[24]{0:T(128)S(1)}, f32[24]{0:T(128)}, u32[]{:S(2)}) copy-start(f32[24]{0:T(128)} %get-tuple-element.50) | copy-start | bytes 292
  938.5 26.6 %copy-start.15 = (f32[24]{0:T(128)S(1)}, f32[24]{0:T(128)}, u32[]{:S(2)}) copy-start(f32[24]{0:T(128)} %get-tuple-element.51) | copy-start | bytes 292
  938.5 26.6 %copy-start.16 = (f32[24]{0:T(128)S(1)}, f32[24]{0:T(128)}, u32[]{:S(2)}) copy-start(f32[24]{0:T(128)} %get-tuple-element.52) | copy-start | bytes 292
  941.5 23.7 %copy-start.20 = (f32[24]{0:T(128)S(1)}, f32[24]{0:T(128)}, u32[]{:S(2)}) copy-start(f32[24]{0:T(128)} %get-tuple-element.56) | copy-start | bytes 292
  941.5 23.7 %copy-start.21 = (f32[24]{0:T(128)S(1)}, f32[24]{0:T(128)}, u32[]{:S(2)}) copy-start(f32[24]{0:T(128)} %get-tuple-element.57) | copy-start | bytes 292
  941.5 23.7 %copy-start.22 = (f32[24]{0:T(128)S(1)}, f32[24]{0:T(128)}, u32[]{:S(2)}) copy-start(f32[24]{0:T(128)} %get-tuple-element.58) | copy-start | bytes 292
  941.6 23.7 %copy-start.23 = (f32[24]{0:T(128)S(1)}, f32[24]{0:T(128)}, u32[]{:S(2)}) copy-start(f32[24]{0:T(128)} %get-tuple-element.59) | copy-start | bytes 292
  941.6 23.7 %copy-start.24 = (f32[24]{0:T(128)S(1)}, f32[24]{0:T(128)}, u32[]{:S(2)}) copy-start(f32[24]{0:T(128)} %get-tuple-element.60) | copy-start | bytes 292
  941.6 23.7 %copy-start.25 = (f32[24]{0:T(128)S(1)}, f32[24]{0:T(128)}, u32[]{:S(2)}) copy-start(f32[24]{0:T(128)} %get-tuple-element.61) | copy-start | bytes 292
  941.6 23.7 %copy-start.26 = (f32[24]{0:T(128)S(1)}, f32[24]{0:T(128)}, u32[]{:S(2)}) copy-start(f32[24]{0:T(128)} %get-tuple-element.62) | copy-start | bytes 292
  941.6 23.7 %copy-start.27 = (f32[24]{0:T(128)S(1)}, f32[24]{0:T(128)}, u32[]{:S(2)}) copy-start(f32[24]{0:T(128)} %get-tuple-element.63) | copy-start | bytes 292
  941.6 23.7 %copy-start.28 = (f32[24]{0:T(128)S(1)}, f32[24]{0:T(128)}, u32[]{:S(2)}) copy-start(f32[24]{0:T(128)} %get-tuple-element.64) | copy-start | bytes 292
  941.7 56.9 %copy-start.45 = (f32[24]{0:T(128)S(1)}, f32[24]{0:T(128)}, u32[]{:S(2)}) copy-start(f32[24]{0:T(128)} %get-tuple-element.88) | copy-start | bytes 292
  941.7 56.9 %copy-start.46 = (f32[24]{0:T(128)S(1)}, f32[24]{0:T(128)}, u32[]{:S(2)}) copy-start(f32[24]{0:T(128)} %get-tuple-element.89) | copy-start | bytes 292
  (29 other events, 467.9 us)
